TPU v7x, 32 devices: a whole 2x2x4 slice. The times are simulated.
32 devices in a mesh: groups: 2 (over y), ctx: 4 (over z), head: 2 (over x), sub: 2 (over core).
Axes of the slice: x: 2, y: 2, z: 4, core: 2. Of those that a mesh axis runs over, the one named last changes fastest.
Arguments:
- queries: bfloat16 [3072, 8192], P(('groups', 'ctx'), ('head', 'sub')), parts along dimension 0, may hold values from -60 to 60
- key_rows: bfloat16 [3072, 1024], P(('groups', 'ctx'), 'head'), parts along dimension 0, may hold values from -6 to 6
- value_rows: bfloat16 [3072, 1024], P(('groups', 'ctx'), 'head'), parts along dimension 0, may hold values from -6 to 6
- out_weight: bfloat16 [8192, 5120], P(('head', 'sub'), 'ctx'), may hold values from -0.375 to 0.375
Outputs:
- mixed: bfloat16 [3072, 5120], P(('groups', 'ctx'), ('head', 'sub')), parts along dimension 0
There are 2 independent parts, one for each index of `groups`. A program takes and returns all parts, laid end to end along the dimension named above; an argument that names none is the same for every part. Nothing has to cross between parts.
All inputs are finite; a program needn't handle non-finite values.
Results may differ from a plain program's by a relative error of at most 0.02.
Values may be sent and summed in bfloat16 or wider, within the bound.
A program may use at most 128 MiB of HBM per device.

v0:
```python
import jax
import jax.numpy as jnp
from jax import lax
from jax.sharding import PartitionSpec as P

QH = 64
KVH = 8
HD = 128


def from_behind(block, axis, distance):
    devices = range(lax.axis_size(axis))
    route = [((i - distance) % len(devices), i) for i in devices]
    return lax.ppermute(block, axis, route)


def on_device(queries, key_rows, value_rows, out_weight):
    token_count = queries.shape[0]
    heads_here = queries.shape[1] // HD
    pairs_here = key_rows.shape[1] // HD
    group_ratio = QH // KVH
    pairs_read = max(heads_here // group_ratio, 1)
    per_pair = heads_here // pairs_read
    head_offset = lax.axis_index("sub") * heads_here // group_ratio
    keys_read = lax.dynamic_slice_in_dim(
        key_rows.reshape(token_count, pairs_here, HD), head_offset, pairs_read, 1
    )
    values_read = lax.dynamic_slice_in_dim(
        value_rows.reshape(token_count, pairs_here, HD), head_offset, pairs_read, 1
    )
    stacked = jnp.stack([keys_read, values_read])
    grouped = queries.reshape(token_count, pairs_read, per_pair, HD)
    factor = 1.0 / HD**0.5

    def absorb(running, key_block, value_block):
        old_max, old_sum, old_out = running
        scores = (
            jnp.einsum("tngd,knd->tngk", grouped, key_block, preferred_element_type=jnp.float32)
            * factor
        )
        new_max = jnp.maximum(old_max, jnp.max(scores, axis=-1))
        shrink = jnp.exp(old_max - new_max)
        expo = jnp.exp(scores - new_max[..., None])
        new_sum = old_sum * shrink + jnp.sum(expo, axis=-1)
        added = jnp.einsum(
            "tngk,knd->tngd",
            expo.astype(jnp.bfloat16),
            value_block,
            preferred_element_type=jnp.float32,
        )
        return (new_max, new_sum, old_out * shrink[..., None] + added)

    empty = (
        jnp.full((token_count, pairs_read, per_pair), -1e30, jnp.float32),
        jnp.zeros((token_count, pairs_read, per_pair), jnp.float32),
        jnp.zeros((token_count, pairs_read, per_pair, HD), jnp.float32),
    )
    cycle_size = lax.axis_size("ctx")

    def forward(blocks):
        return from_behind(blocks, "ctx", 1)

    def both_turn(turn_index, loop_state):
        ahead, behind, running = loop_state
        ahead = forward(ahead)
        behind = from_behind(behind, "ctx", -1)
        running = absorb(running, ahead[0], ahead[1])
        return (ahead, behind, absorb(running, behind[0], behind[1]))

    ahead, _, final = lax.fori_loop(
        0,
        (cycle_size - 1) // 2,
        both_turn,
        (stacked, stacked, absorb(empty, keys_read, values_read)),
    )
    ahead = forward(ahead)
    final = absorb(final, ahead[0], ahead[1])
    attended = (
        (final[2] / final[1][..., None]).astype(jnp.bfloat16).reshape(token_count, heads_here * HD)
    )
    partial_value = jnp.dot(
        attended,
        lax.all_gather(out_weight, "ctx", axis=1, tiled=True),
        preferred_element_type=jnp.float32,
    )
    summed = lax.psum_scatter(
        partial_value.astype(jnp.bfloat16), ("head", "sub"), scatter_dimension=1, tiled=True
    )
    return summed


def solution(mesh):
    return jax.shard_map(
        on_device,
        mesh=mesh,
        in_specs=(
            P(("groups", "ctx"), ("head", "sub")),
            P(("groups", "ctx"), "head"),
            P(("groups", "ctx"), "head"),
            P(("head", "sub"), "ctx"),
        ),
        out_specs=P(("groups", "ctx"), ("head", "sub")),
        check_vma=False,
    )
```

profile of v0, /device:TPU:0, one launch (start us, length us, event | category | flops | bytes accessed | tf_op | source)
XLA Modules:
  0.0 442.7 jit_solution(13286977916574830429)
XLA Ops:
  6.5 0.7 all-gather.2.cloned.1.call-update
  7.3 1.2 copy.17
  8.5 1.2 copy.20
  10.2 3.1 collective-permute-start
  13.3 2.1 collective-permute-start.1
  15.8 1.5 bitcast_reduce_fusion.3
  17.4 8.0 %collective-permute-done = bf16[2,384,2,128]{3,1,2,0:T(8,128)(2,1)S(1)} collective-permute-done((bf16[2,384,2,128]{3,1,2,0:T(8,128)(2,1)S(1)}, bf16[2,384,2,128]{3,1,2,0:T(8,128)(2,1)S(1)}, u32[]{:S(2)}, u32[]{:S(2)}) %collective-permute-start) | collective-permute-done | bytes 393248 | tf_op jit(solution)/shard_map/while/body/eval_jaxpr/ppermute | solution.py:14
  25.4 1.5 bitcast_reduce_fusion.2
  26.8 12.9 %collective-permute-done.1 = bf16[2,384,2,128]{3,1,2,0:T(8,128)(2,1)S(1)} collective-permute-done((bf16[2,384,2,128]{3,1,2,0:T(8,128)(2,1)S(1)}, bf16[2,384,2,128]{3,1,2,0:T(8,128)(2,1)S(1)}, u32[]{:S(2)}, u32[]{:S(2)}) %collective-permute-start.1) | collective-permute-done | bytes 393248 | tf_op jit(solution)/shard_map/while/body/eval_jaxpr/ppermute | solution.py:14
  39.7 5.1 %bitcast_reduce_fusion.1 = (f32[384,2,8]{0,2,1:T(8,128)S(1)}, f32[2,384,384,8]{2,1,3,0:T(8,128)}) fusion(bf16[384,2,8,128]{3,2,1,0:T(8,128)(2,1)S(1)} %bitcast.138, bf16[2,384,2,128]{3,1,2,0:T(8,128)(2,1)S(1)} %collective-permute-done.1), kind=kOutput, calls=%fused_computation.4 | convolution fusion | flops 608692224 | bytes 11231232 | tf_op jit(solution)/shard_map/while/body/eval_jaxpr/tngd,knd->tngk/dot_general | solution.py:38
  44.8 7.7 %collective-permute-done.2 = bf16[2,384,2,128]{3,1,2,0:T(8,128)(2,1)S(1)} collective-permute-done((bf16[2,384,2,128]{3,1,2,0:T(8,128)(2,1)S(1)}, bf16[2,384,2,128]{3,1,2,0:T(8,128)(2,1)S(1)}, u32[]{:S(2)}, u32[]{:S(2)}) %collective-permute-start.2) | collective-permute-done | bytes 393248 | tf_op jit(solution)/shard_map/ppermute | solution.py:14
  52.5 5.1 %bitcast_reduce_fusion = (f32[384,2,8]{0,2,1:T(8,128)S(1)}, f32[2,384,384,8]{2,1,3,0:T(8,128)}) fusion(bf16[384,2,8,128]{3,2,1,0:T(8,128)(2,1)S(1)} %bitcast.139, bf16[2,384,2,128]{3,1,2,0:T(8,128)(2,1)S(1)} %collective-permute-done.2), kind=kOutput, calls=%fused_computation.1 | convolution fusion | flops 608692224 | bytes 11231232 | tf_op jit(solution)/shard_map/tngd,knd->tngk/dot_general | solution.py:38
  57.6 1.6 fusion.4
  59.2 1.6 fusion.6
  60.8 5.3 %fusion.8 = f32[384,2,8]{0,2,1:T(8,128)S(1)} fusion(f32[2,384,384,8]{2,1,3,0:T(8,128)} %get-tuple-element.38, f32[384,2,8]{0,2,1:T(8,128)S(1)} %get-tuple-element.30), kind=kLoop, calls=%fused_computation.16 | loop fusion | flops 7071744 | bytes 9486336 | tf_op jit(solution)/shard_map/while/body/eval_jaxpr/reduce_sum | solution.py:44
  66.1 5.2 %fusion.10 = f32[384,2,8]{0,2,1:T(8,128)S(1)} fusion(f32[2,384,384,8]{2,1,3,0:T(8,128)} %get-tuple-element.36, f32[384,2,8]{0,2,1:T(8,128)S(1)} %get-tuple-element.28), kind=kLoop, calls=%fused_computation.18 | loop fusion | flops 7071744 | bytes 9486336 | tf_op jit(solution)/shard_map/reduce_sum | solution.py:44
  72.0 2.0 fusion.18
  74.2 1.8 fusion.16
  76.1 1.7 fusion.14
  77.9 1.1 slice-done.5
  79.0 3.6 fusion.29
  82.6 296.6 %all-gather.2.cloned.1.call-done = bf16[2048,5120]{1,0:T(8,128)(2,1)} async-done(((bf16[2048,1280]{1,0:T(8,128)(2,1)}), bf16[2048,5120]{1,0:T(8,128)(2,1)}) %all-gather.2.cloned.1.call-update) | async-done | bytes 20971536 | tf_op jit(solution)/shard_map/all_gather | solution.py:83
  379.1 14.5 %convolution_convert_fusion = bf16[384,5120]{1,0:T(8,128)(2,1)} fusion(bf16[384,2048]{0,1:T(8,128)(2,1)} %bitcast.147, bf16[2048,5120]{1,0:T(8,128)(2,1)} %all-gather.2.cloned.1.call-done), kind=kOutput, calls=%fused_computation.20 | convolution fusion | flops 8055029760 | bytes 26476544 | tf_op jit(solution)/shard_map/dot_general | solution.py:81
  393.7 42.2 %reduce-scatter.2.cloned.1.call-done = bf16[384,1280]{1,0:T(8,128)(2,1)} async-done(((bf16[384,5120]{1,0:T(8,128)(2,1)}), bf16[384,1280]{1,0:T(8,128)(2,1)}) %reduce-scatter.2.cloned.1.call-update) | async-done | bytes 983056 | tf_op jit(solution)/shard_map/reduce_scatter | solution.py:86
  (46 shorter events, 1.8 us)
Async XLA Ops:
  6.5 8.9 %copy-start = (bf16[384,2048]{1,0:T(8,128)(2,1)S(1)}, bf16[384,2048]{1,0:T(8,128)(2,1)}, u32[]{:S(2)}) copy-start(bf16[384,2048]{1,0:T(8,128)(2,1)} %param.4) | copy-start | bytes 4718596
  6.5 372.6 %all-gather.2.cloned.1.call-start = ((), (), s32[]{:S(2)}) async-start(), calls=%async_computation.1 | async-start | bytes 26214400 | tf_op jit(solution)/shard_map/all_gather | solution.py:83
  7.3 428.7 %reduce-scatter.2.cloned.1.call-start = ((), (), s32[]{:S(2)}) async-start(), calls=%async_computation.2 | async-start | bytes 4915200 | tf_op jit(solution)/shard_map/reduce_scatter | solution.py:86
  10.2 15.1 %collective-permute-start = (bf16[2,384,2,128]{3,1,2,0:T(8,128)(2,1)S(1)}, bf16[2,384,2,128]{3,1,2,0:T(8,128)(2,1)S(1)}, u32[]{:S(2)}, u32[]{:S(2)}) collective-permute-start(bf16[2,384,2,128]{3,1,2,0:T(8,128)(2,1)S(1)} %pad_maximum_fusion), channel_id=1, source_target_pairs={{12,0},{0,4},{4,8},{8,12},{13,1},{1,5},{5,9},{9,13},{14,2},{2,6},{... | collective-permute-start | bytes 1179656 | tf_op jit(solution)/shard_map/while/body/eval_jaxpr/ppermute | solution.py:14
  13.3 26.4 %collective-permute-start.1 = (bf16[2,384,2,128]{3,1,2,0:T(8,128)(2,1)S(1)}, bf16[2,384,2,128]{3,1,2,0:T(8,128)(2,1)S(1)}, u32[]{:S(2)}, u32[]{:S(2)}) collective-permute-start(bf16[2,384,2,128]{3,1,2,0:T(8,128)(2,1)S(1)} %pad_maximum_fusion), channel_id=1, source_target_pairs={{4,0},{8,4},{12,8},{0,12},{5,1},{9,5},{13,9},{1,13},{6,2},{10,6},{... | collective-permute-start | bytes 1179656 | tf_op jit(solution)/shard_map/while/body/eval_jaxpr/ppermute | solution.py:14
  25.3 19.5 %copy-start.1 = (bf16[2,384,2,128]{3,1,2,0:T(8,128)(2,1)}, bf16[2,384,2,128]{3,1,2,0:T(8,128)(2,1)S(1)}, u32[]{:S(2)}) copy-start(bf16[2,384,2,128]{3,1,2,0:T(8,128)(2,1)S(1)} %collective-permute-done) | copy-start | bytes 1179652
  25.3 27.2 %collective-permute-start.2 = (bf16[2,384,2,128]{3,1,2,0:T(8,128)(2,1)S(1)}, bf16[2,384,2,128]{3,1,2,0:T(8,128)(2,1)S(1)}, u32[]{:S(2)}, u32[]{:S(2)}) collective-permute-start(bf16[2,384,2,128]{3,1,2,0:T(8,128)(2,1)S(1)} %collective-permute-done), channel_id=1, source_target_pairs={{12,0},{0,4},{4,8},{8,12},{13,1},{1,5},{5,9},{9,13},{14,2},{2,6},{... | collective-permute-start | bytes 1179656 | tf_op jit(solution)/shard_map/ppermute | solution.py:14
  39.7 17.9 %copy-start.3 = (bf16[2,384,2,128]{3,1,2,0:T(8,128)(2,1)}, bf16[2,384,2,128]{3,1,2,0:T(8,128)(2,1)S(1)}, u32[]{:S(2)}) copy-start(bf16[2,384,2,128]{3,1,2,0:T(8,128)(2,1)S(1)} %collective-permute-done.1) | copy-start | bytes 1179652
  52.5 6.7 %copy-start.5 = (bf16[2,384,2,128]{3,1,2,0:T(8,128)(2,1)}, bf16[2,384,2,128]{3,1,2,0:T(8,128)(2,1)S(1)}, u32[]{:S(2)}) copy-start(bf16[2,384,2,128]{3,1,2,0:T(8,128)(2,1)S(1)} %collective-permute-done.2) | copy-start | bytes 1179652
  71.4 2.7 copy-start.2
  72.0 3.9 slice-start
  72.0 3.9 slice-start.1
  74.1 1.9 slice-start.2
  74.1 2.0 copy-start.4
  74.1 3.7 slice-start.3
  74.1 3.7 slice-start.4
  76.1 2.9 slice-start.5
  76.1 2.9 copy-start.6
  76.1 2.9 copy-start.7
  76.1 2.9 copy-start.8
  76.1 2.9 copy-start.9
  76.1 2.9 copy-start.10
Sparse Core Ops, SparseCore 0:
  8.9 370.1 all-gather.1
  393.8 42.0 reduce-scatter.1
where the time goes:
time: 443 us
  waiting for transfers between devices  368 us (83%)
  matrix products  36.8 us (8%)
  other arithmetic  14.5 us (3%)
  between operations  13.7 us (3%)
  starting transfers between devices  5.24 us (1%)
  local copies, waits for them, and re-layouts  4.47 us (1%)
    all_gather x1, waiting for transfers between devices, on_device(): lax.all_gather(out_weight, 'ctx', axis=1, tiled=True)  297 us
    reduce_scatter x1, waiting for transfers between devices, on_device(): lax.psum_scatter(partial_value.astype(jnp.bfloat16), ('head', 'sub'), sca...  42.2 us
    ppermute x3, waiting for transfers between devices, from_behind(): return lax.ppermute(block, axis, route)  28.6 us
    dot_general x1, matrix products, on_device(): jnp.dot(attended, lax.all_gather(out_weight, 'ctx', axis=1, tiled=True),...  14.5 us
    reduce_sum x4, other arithmetic, absorb(): new_sum = old_sum * shrink + jnp.sum(expo, axis=-1)  13.7 us
    dot_general x4, matrix products, absorb(): jnp.einsum('tngd,knd->tngk', grouped, key_block, preferred_element_type=j...  13.2 us
    dot_general x4, matrix products, absorb(): jnp.einsum('tngk,knd->tngd', expo.astype(jnp.bfloat16), value_block, pref...  9.13 us
  transfers between devices with their start and end apart: 5, of which 5 were waited for; matrix products, arithmetic and copies ran while one was open for 9% of the time, Pallas kernels for 0%

commit v1 on v0

--- a/solution.py
+++ b/solution.py
@@ -1,3 +1,4 @@
+import functools
 import jax
 import jax.numpy as jnp
 from jax import lax
@@ -6,6 +7,21 @@
 QH = 64
 KVH = 8
 HD = 128
+
+
+def push_patch(local_values, at_axis):
+    n_parts = lax.psum(1, axis_name="ctx")
+    seen = [n_parts if c == at_axis else 1 for c in range(local_values.ndim)]
+    return lax.all_to_all(
+        jnp.tile(local_values, seen),
+        tiled=True,
+        split_axis=at_axis,
+        concat_axis=at_axis,
+        axis_name="ctx",
+    )
+
+
+mark_the_samples_all = functools.partial(push_patch, at_axis=1)
 
 
 def from_behind(block, axis, distance):
@@ -79,9 +95,7 @@
         (final[2] / final[1][..., None]).astype(jnp.bfloat16).reshape(token_count, heads_here * HD)
     )
     partial_value = jnp.dot(
-        attended,
-        lax.all_gather(out_weight, "ctx", axis=1, tiled=True),
-        preferred_element_type=jnp.float32,
+        attended, mark_the_samples_all(out_weight), preferred_element_type=jnp.float32
     )
     summed = lax.psum_scatter(
         partial_value.astype(jnp.bfloat16), ("head", "sub"), scatter_dimension=1, tiled=True

time: 443 us -> 633 us (1.43)
  starting transfers between devices: 5.24 us -> 123 us
  waiting for transfers between devices: 368 us -> 402 us
  local copies, waits for them, and re-layouts: 4.47 us -> 37.5 us
    ppermute x3, waiting for transfers between devices: 28.6 us -> 353 us  [from_behind(): return lax.ppermute(block, axis, route)]
    all_gather x1 -> x0, waiting for transfers between devices: 297 us -> none  [on_device(): lax.all_gather(out_weight, 'ctx', axis=1, tiled=True)]
    ppermute x3, starting transfers between devices: 5.2 us -> 115 us  [from_behind(): return lax.ppermute(block, axis, route)]
    all_to_all x0 -> x1, local copies, waits for them, and re-layouts: none -> 27.2 us  [push_patch(): lax.all_to_all(jnp.tile(local_values, seen), tiled=True, split_axis=at_ax...]
    another operation x0 -> x1, local copies, waits for them, and re-layouts: none -> 9.06 us  [push_patch(): jnp.tile(local_values, seen)]
    all_to_all x0 -> x1, starting transfers between devices: none -> 7.85 us  [push_patch(): lax.all_to_all(jnp.tile(local_values, seen), tiled=True, split_axis=at_ax...]
    dot_general x4, matrix products: 9.13 us -> 15.5 us  [absorb(): jnp.einsum('tngk,knd->tngd', expo.astype(jnp.bfloat16), value_block, pref...]
  transfers between devices with their start and end apart: 5 -> 5, of which waited for: 5 -> 3; matrix products, arithmetic and copies ran while one was open for 9% -> 7% of each run, Pallas kernels for 0% -> 0%
where the time goes in v1:
time: 633 us; the launch traced here: 632 us
  waiting for transfers between devices  402 us (64%)
  starting transfers between devices  123 us (19%)
  matrix products  42.6 us (7%)
  local copies, waits for them, and re-layouts  37.5 us (6%)
  other arithmetic  13.8 us (2%)
  between operations  13.6 us (2%)
    ppermute x3, waiting for transfers between devices, from_behind(): return lax.ppermute(block, axis, route)  353 us
    ppermute x3, starting transfers between devices, from_behind(): return lax.ppermute(block, axis, route)  115 us
    reduce_scatter x1, waiting for transfers between devices, on_device(): lax.psum_scatter(partial_value.astype(jnp.bfloat16), ('head', 'sub'), sca...  48.3 us
    all_to_all x1, local copies, waits for them, and re-layouts, push_patch(): lax.all_to_all(jnp.tile(local_values, seen), tiled=True, split_axis=at_ax...  27.2 us
    dot_general x4, matrix products, absorb(): jnp.einsum('tngk,knd->tngd', expo.astype(jnp.bfloat16), value_block, pref...  15.5 us
    dot_general x1, matrix products, on_device(): jnp.dot(attended, mark_the_samples_all(out_weight), preferred_element_typ...  13.9 us
    reduce_sum x4, other arithmetic, absorb(): new_sum = old_sum * shrink + jnp.sum(expo, axis=-1)  13.7 us
    dot_general x4, matrix products, absorb(): jnp.einsum('tngd,knd->tngk', grouped, key_block, preferred_element_type=j...  13.2 us
  transfers between devices with their start and end apart: 5, of which 3 were waited for; matrix products, arithmetic and copies ran while one was open for 7% of the time, Pallas kernels for 0%

profile of v1, /device:TPU:0, one launch (start us, length us, event | category | flops | bytes accessed | tf_op | source)
XLA Modules:
  0.0 631.7 jit_solution(13459318429761866275)
XLA Ops:
  6.5 9.1 %tile.2 = bf16[2048,4,1280]{2,0,1:T(8,128)(2,1)} broadcast(bf16[2048,1280]{1,0:T(8,128)(2,1)} %param.7), dimensions={0,2} | broadcast | bytes 26214400 | tf_op jit(solution)/shard_map/tile | solution.py:16
  15.6 7.9 %all-to-all-start = ((bf16[2048,4,1280]{2,0,1:T(8,128)(2,1)}), bf16[2048,4,1280]{2,0,1:T(8,128)(2,1)}, u32[]{:S(2)}, u32[]{:S(2)}) async-start(bf16[2048,4,1280]{2,0,1:T(8,128)(2,1)} %tile.2), calls=%async_computation | async-start | bytes 41943040 | tf_op jit(solution)/shard_map/all_to_all | solution.py:15
  23.5 0.2 copy.47
  23.8 0.2 copy.50
  24.4 5.0 collective-permute-start.1
  29.5 0.4 copy.82
  29.9 1.5 bitcast_reduce_fusion.3
  31.4 352.0 %collective-permute-done = bf16[2,384,2,128]{3,1,2,0:T(8,128)(2,1)S(1)} collective-permute-done((bf16[2,384,2,128]{3,1,2,0:T(8,128)(2,1)S(1)}, bf16[2,384,2,128]{3,1,2,0:T(8,128)(2,1)S(1)}, u32[]{:S(2)}, u32[]{:S(2)}) %collective-permute-start) | collective-permute-done | bytes 393248 | tf_op jit(solution)/shard_map/while/body/eval_jaxpr/ppermute | solution.py:30
  383.4 109.8 %collective-permute-start.2 = (bf16[2,384,2,128]{3,1,2,0:T(8,128)(2,1)S(1)}, bf16[2,384,2,128]{3,1,2,0:T(8,128)(2,1)S(1)}, u32[]{:S(2)}, u32[]{:S(2)}) collective-permute-start(bf16[2,384,2,128]{3,1,2,0:T(8,128)(2,1)S(1)} %collective-permute-done), channel_id=1, source_target_pairs={{12,0},{0,4},{4,8},{8,12},{13,1},{1,5},{5,9},{9,13},{14,2},{2,6},{... | collective-permute-start | bytes 1179656 | tf_op jit(solution)/shard_map/ppermute | solution.py:30
  493.2 1.5 bitcast_reduce_fusion.2
  494.7 5.1 bitcast_reduce_fusion.1
  499.8 1.2 collective-permute-done.2
  501.0 5.1 bitcast_reduce_fusion
  506.1 1.6 fusion.4
  507.7 5.3 fusion.10
  513.0 5.3 fusion.8
  518.3 1.6 fusion.6
  519.9 2.1 fusion.18
  521.9 5.4 fusion.14
  527.4 1.7 fusion.16
  529.1 6.3 fusion.29
  535.5 27.2 %copy.62 = bf16[2048,4,1280]{0,2,1:T(8,128)(2,1)} copy(bf16[2048,4,1280]{2,0,1:T(8,128)(2,1)} %all-to-all-done) | data formatting | bytes 41943040 | tf_op jit(solution)/shard_map/all_to_all | solution.py:15
  562.7 13.9 %convolution_convert_fusion = bf16[384,5120]{1,0:T(8,128)(2,1)} fusion(bf16[384,2048]{0,1:T(8,128)(2,1)S(1)} %bitcast.145, bf16[2048,5120]{0,1:T(8,128)(2,1)} %bitcast.139), kind=kOutput, calls=%fused_computation.20 | convolution fusion | flops 8055029760 | bytes 26476544 | tf_op jit(solution)/shard_map/dot_general | solution.py:97
  576.6 48.3 %reduce-scatter.2.cloned.1.call-done = bf16[384,1280]{1,0:T(8,128)(2,1)} async-done(((bf16[384,5120]{1,0:T(8,128)(2,1)}), bf16[384,1280]{1,0:T(8,128)(2,1)}) %reduce-scatter.2.cloned.1.call-update) | async-done | bytes 983056 | tf_op jit(solution)/shard_map/reduce_scatter | solution.py:100
  (17 shorter events, 0.6 us)
Async XLA Ops:
  15.6 7.9 %copy-start.1 = (bf16[384,512]{1,0:T(8,128)(2,1)S(1)}, bf16[384,512]{1,0:T(8,128)(2,1)}, u32[]{:S(2)}) copy-start(bf16[384,512]{1,0:T(8,128)(2,1)} %param.5) | copy-start | bytes 1179652
  15.6 8.2 %copy-start.2 = (bf16[384,512]{1,0:T(8,128)(2,1)S(1)}, bf16[384,512]{1,0:T(8,128)(2,1)}, u32[]{:S(2)}) copy-start(bf16[384,512]{1,0:T(8,128)(2,1)} %param.6) | copy-start | bytes 1179652
  15.6 13.9 %copy-start = (bf16[384,2048]{1,0:T(8,128)(2,1)S(1)}, bf16[384,2048]{1,0:T(8,128)(2,1)}, u32[]{:S(2)}) copy-start(bf16[384,2048]{1,0:T(8,128)(2,1)} %param.4) | copy-start | bytes 4718596
  15.6 519.9 %all-to-all-start = ((bf16[2048,4,1280]{2,0,1:T(8,128)(2,1)}), bf16[2048,4,1280]{2,0,1:T(8,128)(2,1)}, u32[]{:S(2)}, u32[]{:S(2)}) async-start(bf16[2048,4,1280]{2,0,1:T(8,128)(2,1)} %tile.2), calls=%async_computation | async-start | bytes 41943040 | tf_op jit(solution)/shard_map/all_to_all | solution.py:15
  23.5 601.4 %reduce-scatter.2.cloned.1.call-start = ((), (), s32[]{:S(2)}) async-start(), calls=%async_computation.2 | async-start | bytes 4915200 | tf_op jit(solution)/shard_map/reduce_scatter | solution.py:100
  24.4 470.3 %collective-permute-start.1 = (bf16[2,384,2,128]{3,1,2,0:T(8,128)(2,1)S(1)}, bf16[2,384,2,128]{3,1,2,0:T(8,128)(2,1)S(1)}, u32[]{:S(2)}, u32[]{:S(2)}) collective-permute-start(bf16[2,384,2,128]{3,1,2,0:T(8,128)(2,1)S(1)} %pad_maximum_fusion), channel_id=1, source_target_pairs={{4,0},{8,4},{12,8},{0,12},{5,1},{9,5},{13,9},{1,13},{6,2},{10,6},{... | collective-permute-start | bytes 1179656 | tf_op jit(solution)/shard_map/while/body/eval_jaxpr/ppermute | solution.py:30
  29.5 353.9 %collective-permute-start = (bf16[2,384,2,128]{3,1,2,0:T(8,128)(2,1)S(1)}, bf16[2,384,2,128]{3,1,2,0:T(8,128)(2,1)S(1)}, u32[]{:S(2)}, u32[]{:S(2)}) collective-permute-start(bf16[2,384,2,128]{3,1,2,0:T(8,128)(2,1)S(1)} %pad_maximum_fusion), channel_id=1, source_target_pairs={{12,0},{0,4},{4,8},{8,12},{13,1},{1,5},{5,9},{9,13},{14,2},{2,6},{... | collective-permute-start | bytes 1179656 | tf_op jit(solution)/shard_map/while/body/eval_jaxpr/ppermute | solution.py:30
  383.4 117.6 %collective-permute-start.2 = (bf16[2,384,2,128]{3,1,2,0:T(8,128)(2,1)S(1)}, bf16[2,384,2,128]{3,1,2,0:T(8,128)(2,1)S(1)}, u32[]{:S(2)}, u32[]{:S(2)}) collective-permute-start(bf16[2,384,2,128]{3,1,2,0:T(8,128)(2,1)S(1)} %collective-permute-done), channel_id=1, source_target_pairs={{12,0},{0,4},{4,8},{8,12},{13,1},{1,5},{5,9},{9,13},{14,2},{2,6},{... | collective-permute-start | bytes 1179656 | tf_op jit(solution)/shard_map/ppermute | solution.py:30
Sparse Core Ops, SparseCore 0:
  576.7 48.1 reduce-scatter.1
